TPU v7x, 256 devices: a whole 4x4x8 slice. The times are simulated.
256 devices in a mesh: dp: 32 (over y, z), vocab: 8 (over x, core).
Axes of the slice: x: 4, y: 4, z: 8, core: 2. Of those that a mesh axis runs over, the one named last changes fastest.
Arguments:
- draft_logits: bfloat16 [4096, 128000], P('dp', 'vocab'), may hold values from -15 to 250
- hidden: bfloat16 [4096, 2304], P('dp'), may hold values from -40 to 40
- embed_cot: bfloat16 [4096, 2304], P('dp'), may hold values from -0.59765625 to 0.59765625
- draft_ids: int32 [4096], P('dp'), may hold values from 0 to 127999, as said below
- target_ids: int32 [4096, 32], P('dp'), may hold values from 0 to 128255
- target_logits: float32 [4096, 32], P('dp'), may hold values from -8 to 240
- vocab_map: int32 [128256], replicated, may hold values from 0 to 127999
- master: float32 [128000, 2304], P(('vocab', 'dp')), may hold values from -6 to 6
- row_moment: float32 [128000], P(('vocab', 'dp')), may hold values from 0.0001 to 0.5
- col_moment: float32 [2304], replicated, may hold values from 0.003 to 0.03
Outputs:
- direction: bfloat16 [128000, 2304], P(('vocab', 'dp'))
- row_new: float32 [128000], P(('vocab', 'dp'))
- col_new: float32 [2304], replicated
- next_rows: bfloat16 [4096, 2304], P('dp')
Inputs may be any that keep to these rules, and one draw needn't show every extreme that they name: `draft_ids`: among the 128 tokens of one index of dp, at most 20 have draft ids in any one block of 16000 consecutive ids, and some block holds exactly 20 of them.
All inputs are finite; a program needn't handle non-finite values.
Results may differ from a plain program's by a relative error of at most 0.0073.
Values may be sent and summed in bfloat16 or wider, within the bound.
No kernel may reach another device: no remote copies, remote signals or barrier semaphores. Data moves between devices by JAX's collectives and lax.ppermute only.
A program may use at most 128 MiB of HBM per device.

v0:
```python
import jax
import jax.numpy as jnp
from jax import lax
from jax.sharding import PartitionSpec as P

DECAY_RATE = 0.9
STEP_SCALE = 0.01
SQUARE_EPS = 1e-30


def body(
    draft_logits,
    hidden,
    embed_cot,
    draft_ids,
    target_ids,
    target_logits,
    vocab_map,
    master,
    row_moment,
    col_moment,
):
    tokens_here, shard_cols = draft_logits.shape
    owned_rows, features = master.shape
    dp_count = lax.axis_size("dp")
    vocab_count = lax.axis_size("vocab")
    vocab_index = lax.axis_index("vocab")
    dp_index = lax.axis_index("dp")
    logits = draft_logits.astype(jnp.float32)
    local_max = jnp.max(logits, axis=1)
    highest = lax.pmax(local_max, "vocab")
    totals = lax.psum(jnp.sum(jnp.exp(logits - highest[:, None]), axis=1), "vocab")
    probs = jnp.exp(logits - highest[:, None]) / totals[:, None]
    shifted = target_logits - jnp.max(target_logits, axis=1, keepdims=True)
    target_exp = jnp.exp(shifted)
    weights = target_exp / jnp.sum(target_exp, axis=1, keepdims=True)
    mapped = vocab_map[target_ids] - vocab_index * shard_cols
    inside = (mapped >= 0) & (mapped < shard_cols)
    token_index = jnp.broadcast_to(
        jnp.arange(tokens_here, dtype=jnp.int32)[:, None], target_ids.shape
    )
    target = (
        jnp.zeros((tokens_here, shard_cols), jnp.float32)
        .at[token_index, jnp.clip(mapped, 0, shard_cols - 1)]
        .add(jnp.where(inside, weights, jnp.zeros_like(weights)))
    )
    slopes = (probs - target).astype(jnp.bfloat16)
    owned_slopes = lax.all_to_all(slopes, "dp", split_axis=1, concat_axis=0, tiled=True)
    head_grad = jnp.einsum(
        "tv,td->vd",
        owned_slopes,
        lax.all_gather(hidden, "dp", axis=0, tiled=True),
        preferred_element_type=jnp.float32,
    )
    block_base = vocab_index * shard_cols
    in_shard = (draft_ids >= block_base) & (draft_ids < block_base + shard_cols)
    slot_count = tokens_here // vocab_count + tokens_here // (4 * vocab_count)
    position = jnp.cumsum(in_shard.astype(jnp.int32)) - 1
    placing = (position[None, :] == jnp.arange(slot_count, dtype=jnp.int32)[:, None]) & in_shard[
        None, :
    ]
    filled = jnp.any(placing, axis=1)
    packed_ids = jnp.where(filled, jnp.sum(jnp.where(placing, draft_ids[None, :], 0), axis=1), -1)
    placing_half = placing.astype(jnp.bfloat16)
    packed_cot = jnp.dot(placing_half, embed_cot, preferred_element_type=jnp.float32).astype(
        jnp.bfloat16
    )
    all_ids, all_cot = (
        lax.all_gather(packed_ids, "dp", axis=0, tiled=True),
        lax.all_gather(packed_cot, "dp", axis=0, tiled=True),
    )
    row_base = (vocab_index * dp_count + dp_index) * owned_rows
    row_iota = jnp.arange(owned_rows, dtype=jnp.int32)
    matches = (all_ids[None, :] - row_base == row_iota[:, None]).astype(jnp.bfloat16)
    grad = head_grad + jnp.dot(matches, all_cot, preferred_element_type=jnp.float32)
    squares = grad * grad + SQUARE_EPS
    row_new = DECAY_RATE * row_moment + (1.0 - DECAY_RATE) * jnp.mean(squares, axis=1)
    column_total, row_total = lax.psum(
        (jnp.sum(squares, axis=0), jnp.sum(row_new)), ("dp", "vocab")
    )
    vocab_rows = owned_rows * dp_count * vocab_count
    col_new = DECAY_RATE * col_moment + (1.0 - DECAY_RATE) * (column_total / vocab_rows)
    scale = row_new[:, None] * col_new[None, :] / (row_total / vocab_rows)
    direction = grad / jnp.sqrt(scale)
    fresh = (master - STEP_SCALE * direction).astype(jnp.bfloat16)
    wanted = all_ids - row_base
    select = (wanted[:, None] == row_iota[None, :]).astype(jnp.bfloat16)
    slot_values = lax.psum_scatter(
        jnp.dot(select, fresh, preferred_element_type=jnp.float32).astype(jnp.bfloat16),
        "dp",
        scatter_dimension=0,
        tiled=True,
    )
    spread = jnp.einsum("st,sd->td", placing_half, slot_values, preferred_element_type=jnp.float32)
    next_rows = lax.psum(spread.astype(jnp.bfloat16), "vocab")
    return (direction.astype(jnp.bfloat16), row_new, col_new, next_rows)


def solution(mesh):
    in_specs = (
        P("dp", "vocab"),
        P("dp", None),
        P("dp", None),
        P("dp"),
        P("dp", None),
        P("dp", None),
        P(),
        P(("vocab", "dp"), None),
        P(("vocab", "dp")),
        P(),
    )
    out_specs = (P(("vocab", "dp"), None), P(("vocab", "dp")), P(), P("dp", None))
    return jax.shard_map(body, mesh=mesh, in_specs=in_specs, out_specs=out_specs, check_vma=False)
```

profile of v0, /device:TPU:8, one launch (start us, length us, event | category | flops | bytes accessed | tf_op | source)
XLA Modules:
  0.0 619.0 jit_solution(5468428876925927025)
XLA Ops:
  11.0 23.0 %gather_fusion = s32[4096]{0:T(1024)S(1)} fusion(s32[128256]{0:T(1024)S(1)} %copy-done.2, s32[4096]{0:T(1024)S(1)} %broadcast_clamp_fusion), kind=kCustom, calls=%fused_computation | custom fusion | bytes 49152 | tf_op jit(solution)/shard_map/gather | solution.py:37
  35.2 31.6 %scatter_custom_fusion = f32[2048000]{0:T(1024)} fusion(s32[4096]{0:T(1024)S(1)} %reshape.100, f32[4096]{0:T(1024)S(1)} %reshape.102, f32[]{:T(128)} %constant.21.clone.1), kind=kCustom, calls=%fused_computation.10 | custom fusion | flops 4096 | bytes 8192004
  66.8 9.1 %reshape.90 = f32[128,16000]{1,0:T(8,128)} reshape(f32[2048000]{0:T(1024)} %scatter_custom_fusion) | data formatting | bytes 16384000 | tf_op jit(solution)/shard_map/scatter-add | solution.py:45
  78.8 13.1 %pmax.7 = f32[128]{0:T(128)S(1)} all-reduce(bf16[128]{0:T(256)(128)(2,1)S(1)} %reduce_max.23), channel_id=1, replica_groups=mesh['dp'=32,'vocab'=8] {'vocab'}, use_global_device_ids=true, to_apply=%region_1.0 | all-reduce | flops 128 | bytes 768 | tf_op jit(solution)/shard_map/pmax | solution.py:31
  91.9 3.7 fusion.1
  95.5 12.4 %psum.28 = f32[128]{0:T(128)S(1)} all-reduce(f32[128]{0:T(128)S(1)} %fusion.1), channel_id=1, replica_groups=mesh['dp'=32,'vocab'=8] {'vocab'}, use_global_device_ids=true, to_apply=%region_3.0 | all-reduce | flops 128 | bytes 1024 | tf_op jit(solution)/shard_map/psum | solution.py:32
  108.0 6.9 %subtract_convert_fusion = bf16[128,16000]{1,0:T(8,128)(2,1)} fusion(f32[128,16000]{1,0:T(8,128)} %reshape.90, bf16[128,16000]{1,0:T(8,128)(2,1)} %param.10, f32[128]{0:T(128)S(1)} %psum.28, f32[128]{0:T(128)S(1)} %pmax.7), kind=kLoop, calls=%fused_computation.2 | loop fusion | flops 10240000 | bytes 16385024 | tf_op jit(solution)/shard_map/convert_element_type | solution.py:47
  114.9 10.9 %reshape.126 = bf16[128,32,500]{2,1,0:T(8,128)(2,1)} reshape(bf16[128,16000]{1,0:T(8,128)(2,1)} %subtract_convert_fusion) | data formatting | bytes 8192000 | tf_op jit(solution)/shard_map/all_to_all | solution.py:48
  125.7 7.9 %copy.40 = bf16[128,32,500]{0,2,1:T(8,128)(2,1)} copy(bf16[128,32,500]{2,1,0:T(8,128)(2,1)} %reshape.126) | data formatting | bytes 8192000 | tf_op jit(solution)/shard_map/all_to_all | solution.py:48
  133.6 11.5 %all-to-all-start = ((bf16[128,32,500]{0,2,1:T(8,128)(2,1)}), bf16[128,32,500]{0,2,1:T(8,128)(2,1)}, u32[]{:S(2)}, u32[]{:S(2)}) async-start(bf16[128,32,500]{0,2,1:T(8,128)(2,1)} %copy.40), calls=%async_computation | async-start | bytes 8257536 | tf_op jit(solution)/shard_map/all_to_all | solution.py:48
  146.8 146.2 %all-reduce = s32[640]{0:T(1024)S(1)} all-reduce(s32[640]{0:T(1024)S(1)} %select_dynamic-update-slice_fusion), channel_id=1, replica_groups=mesh['dp'=32,'vocab'=8] {'dp'}, use_global_device_ids=true, to_apply=%add | all-reduce | flops 640 | bytes 5120
  293.0 3.8 reshape.123
  296.8 4.1 fusion.8
  301.0 6.6 %copy.38 = bf16[32,128,500]{2,1,0:T(8,128)(2,1)} copy(bf16[32,128,500]{1,2,0:T(8,128)(2,1)} %bitcast) | data formatting | bytes 8192000 | tf_op jit(solution)/shard_map/all_to_all | solution.py:48
  307.5 18.4 %all-gather.4.cloned.1.call-done = bf16[4096,2304]{1,0:T(8,128)(2,1)} async-done(((bf16[128,2304]{1,0:T(8,128)(2,1)}), bf16[4096,2304]{1,0:T(8,128)(2,1)}) %all-gather.4.cloned.1.call-update) | async-done | bytes 18874384 | tf_op jit(solution)/shard_map/all_gather | solution.py:52
  326.0 18.5 %fusion.4 = (f32[2304]{0:T(1024)S(1)}, f32[500]{0:T(512)S(1)}, f32[500,2304]{1,0:T(8,128)}) fusion(f32[500,2304]{1,0:T(8,128)} %fusion.8, bf16[4096,500]{1,0:T(8,128)(2,1)} %bitcast.14, bf16[4096,2304]{1,0:T(8,128)(2,1)} %all-gather.4.cloned.1.call-done), kind=kOutput, calls=%fused_computation.12 | convolution fusion | flops 9442941952 | bytes 32197584 | tf_op jit(solution)/shard_map/tv,td->vd/dot_general | solution.py:49
  345.1 74.8 %all-reduce.3 = (f32[]{:T(128)}, f32[2304]{0:T(1024)S(1)}) all-reduce(f32[]{:T(128)} %get-tuple-element.8, f32[2304]{0:T(1024)S(1)} %get-tuple-element.4), channel_id=1, replica_groups=mesh['dp'=32,'vocab'=8] {'dp','vocab'}, use_global_device_ids=true, to_apply=%region_14.15 | all-reduce | flops 2305 | bytes 18440 | tf_op jit(solution)/shard_map/psum | solution.py:78
  420.6 5.8 convolution_convert_fusion
  426.4 79.6 %fusion = bf16[24,2304]{1,0:T(8,128)(2,1)S(1)} fusion(bf16[640,2304]{1,0:T(8,128)(2,1)S(1)} %convolution_convert_fusion), kind=kCustom, calls=%all-reduce-scatter | all-reduce-scatter fusion | flops 1769473 | bytes 3060736
  510.2 4.7 collective-permute-start.1
  518.1 7.8 %collective-permute-start.3 = (bf16[24,2304]{1,0:T(8,128)(2,1)S(1)}, bf16[24,2304]{1,0:T(8,128)(2,1)S(1)}, u32[]{:S(2)}, u32[]{:S(2)}) collective-permute-start(bf16[24,2304]{1,0:T(8,128)(2,1)S(1)} %fusion), channel_id=1, source_target_pairs={{0,32},{8,40},{16,48},{24,56},{32,64},{40,72},{48,80},{56,88},{64,... | collective-permute-start | bytes 331784
  526.0 8.8 %collective-permute-start.4 = (bf16[24,2304]{1,0:T(8,128)(2,1)S(1)}, bf16[24,2304]{1,0:T(8,128)(2,1)S(1)}, u32[]{:S(2)}, u32[]{:S(2)}) collective-permute-start(bf16[24,2304]{1,0:T(8,128)(2,1)S(1)} %fusion), channel_id=1, source_target_pairs={{0,40},{8,48},{16,56},{24,64},{32,72},{40,80},{48,88},{56,96},{64,... | collective-permute-start | bytes 331784
  541.1 4.5 fusion.23
  545.6 64.9 %all-reduce.6.cloned.1.call-done = bf16[128,2304]{1,0:T(8,128)(2,1)} async-done(((bf16[128,2304]{1,0:T(8,128)(2,1)}), bf16[128,2304]{1,0:T(8,128)(2,1)}) %all-reduce.6.cloned.1.call-update) | async-done | bytes 589840 | tf_op jit(solution)/shard_map/psum | solution.py:95
  (86 shorter events, 24.3 us)
Async XLA Ops:
  7.2 3.8 copy-start.2
  7.2 285.8 %all-gather.6.cloned.1.call-start = ((), (), s32[]{:S(2)}) async-start(), calls=%async_computation.3 | async-start | bytes 3649536 | tf_op jit(solution)/shard_map/all_gather | solution.py:70
  8.0 138.6 %copy-start.9 = (pred[128]{0:T(512)(128)(4,1)}, pred[128]{0:T(512)(128)(4,1)S(1)}, u32[]{:S(2)}) copy-start(pred[128]{0:T(512)(128)(4,1)S(1)} %get-tuple-element.11) | copy-start | bytes 388
  8.4 138.2 %copy-start.8 = (s32[128]{0:T(128)}, s32[128]{0:T(128)S(1)}, u32[]{:S(2)}) copy-start(s32[128]{0:T(128)S(1)} %add_reduce_fusion) | copy-start | bytes 1540
  9.3 316.7 %all-gather.4.cloned.1.call-start = ((), (), s32[]{:S(2)}) async-start(), calls=%async_computation.1 | async-start | bytes 19464192 | tf_op jit(solution)/shard_map/all_gather | solution.py:52
  11.0 23.3 %copy-start.14 = (s32[2]{0:T(128)S(1)}, s32[2]{0:T(128)}, u32[]{:S(2)}) copy-start(s32[2]{0:T(128)} %constant.64) | copy-start | bytes 28
  11.0 23.3 %copy-start.13 = (s32[2]{0:T(128)S(1)}, s32[2]{0:T(128)}, u32[]{:S(2)}) copy-start(s32[2]{0:T(128)} %constant.67) | copy-start | bytes 28
  11.0 23.7 %copy-start.4 = (f32[128,32]{0,1:T(8,128)S(1)}, f32[128,32]{0,1:T(8,128)}, u32[]{:S(2)}) copy-start(f32[128,32]{0,1:T(8,128)} %param.15) | copy-start | bytes 49156
  133.6 11.6 %copy-start.12 = (u32[256]{0:T(256)S(1)}, u32[256]{0:T(256)}, u32[]{:S(2)}) copy-start(u32[256]{0:T(256)} %constant.74) | copy-start | bytes 3076
  133.6 13.0 %copy-start.11 = (s32[128]{0:T(128)S(1)}, s32[128]{0:T(128)}, u32[]{:S(2)}) copy-start(s32[128]{0:T(128)} %param.13) | copy-start | bytes 1540
  133.6 167.3 %all-to-all-start = ((bf16[128,32,500]{0,2,1:T(8,128)(2,1)}), bf16[128,32,500]{0,2,1:T(8,128)(2,1)}, u32[]{:S(2)}, u32[]{:S(2)}) async-start(bf16[128,32,500]{0,2,1:T(8,128)(2,1)} %copy.40), calls=%async_computation | async-start | bytes 8257536 | tf_op jit(solution)/shard_map/all_to_all | solution.py:48
  145.2 465.4 %all-reduce.6.cloned.1.call-start = ((), (), s32[]{:S(2)}) async-start(), calls=%async_computation.2 | async-start | bytes 1179648 | tf_op jit(solution)/shard_map/psum | solution.py:95
  326.0 18.5 %copy-start.10 = (f32[500]{0:T(512)S(1)}, f32[500]{0:T(512)}, u32[]{:S(2)}) copy-start(f32[500]{0:T(512)} %param.18) | copy-start | bytes 6004
  326.0 94.0 %copy-start.6 = (f32[2304]{0:T(1024)S(1)}, f32[2304]{0:T(1024)}, u32[]{:S(2)}) copy-start(f32[2304]{0:T(1024)} %param.19) | copy-start | bytes 27652
  345.1 196.0 %copy-start.7 = (f32[500]{0:T(512)}, f32[500]{0:T(512)S(1)}, u32[]{:S(2)}) copy-start(f32[500]{0:T(512)S(1)} %get-tuple-element.16) | copy-start | bytes 6004
  420.0 121.1 %copy-start.5 = (f32[2304]{0:T(1024)}, f32[2304]{0:T(1024)S(1)}, u32[]{:S(2)}) copy-start(f32[2304]{0:T(1024)S(1)} %multiply_add_fusion.1) | copy-start | bytes 27652
  506.1 29.4 %copy-start.3 = (bf16[24,2304]{1,0:T(8,128)(2,1)}, bf16[24,2304]{1,0:T(8,128)(2,1)S(1)}, u32[]{:S(2)}) copy-start(bf16[24,2304]{1,0:T(8,128)(2,1)S(1)} %fusion) | copy-start | bytes 331780
  506.1 19.9 %collective-permute-start.5 = (bf16[4,2304]{1,0:T(4,128)(2,1)S(1)}, bf16[4,2304]{1,0:T(4,128)(2,1)S(1)}, u32[]{:S(2)}, u32[]{:S(2)}) collective-permute-start(bf16[4,2304]{1,0:T(4,128)(2,1)S(1)} %slice.2), channel_id=1, source_target_pairs={{0,48},{8,56},{16,64},{24,72},{32,80},{40,88},{48,96},{56,104},{64... | collective-permute-start | bytes 55304
  508.0 27.4 %collective-permute-start = (bf16[24,2304]{1,0:T(8,128)(2,1)S(1)}, bf16[24,2304]{1,0:T(8,128)(2,1)S(1)}, u32[]{:S(2)}, u32[]{:S(2)}) collective-permute-start(bf16[24,2304]{1,0:T(8,128)(2,1)S(1)} %fusion), channel_id=1, source_target_pairs={{0,8},{8,16},{16,24},{24,32},{32,40},{40,48},{48,56},{56,64},{64,7... | collective-permute-start | bytes 331784
  510.2 25.3 %collective-permute-start.1 = (bf16[24,2304]{1,0:T(8,128)(2,1)S(1)}, bf16[24,2304]{1,0:T(8,128)(2,1)S(1)}, u32[]{:S(2)}, u32[]{:S(2)}) collective-permute-start(bf16[24,2304]{1,0:T(8,128)(2,1)S(1)} %fusion), channel_id=1, source_target_pairs={{0,16},{8,24},{16,32},{24,40},{32,48},{40,56},{48,64},{56,72},{64,... | collective-permute-start | bytes 331784
  514.9 20.6 %collective-permute-start.2 = (bf16[24,2304]{1,0:T(8,128)(2,1)S(1)}, bf16[24,2304]{1,0:T(8,128)(2,1)S(1)}, u32[]{:S(2)}, u32[]{:S(2)}) collective-permute-start(bf16[24,2304]{1,0:T(8,128)(2,1)S(1)} %fusion), channel_id=1, source_target_pairs={{0,24},{8,32},{16,40},{24,48},{32,56},{40,64},{48,72},{56,80},{64,... | collective-permute-start | bytes 331784
  518.1 17.3 %collective-permute-start.3 = (bf16[24,2304]{1,0:T(8,128)(2,1)S(1)}, bf16[24,2304]{1,0:T(8,128)(2,1)S(1)}, u32[]{:S(2)}, u32[]{:S(2)}) collective-permute-start(bf16[24,2304]{1,0:T(8,128)(2,1)S(1)} %fusion), channel_id=1, source_target_pairs={{0,32},{8,40},{16,48},{24,56},{32,64},{40,72},{48,80},{56,88},{64,... | collective-permute-start | bytes 331784
  526.0 11.1 %collective-permute-start.4 = (bf16[24,2304]{1,0:T(8,128)(2,1)S(1)}, bf16[24,2304]{1,0:T(8,128)(2,1)S(1)}, u32[]{:S(2)}, u32[]{:S(2)}) collective-permute-start(bf16[24,2304]{1,0:T(8,128)(2,1)S(1)} %fusion), channel_id=1, source_target_pairs={{0,40},{8,48},{16,56},{24,64},{32,72},{40,80},{48,88},{56,96},{64,... | collective-permute-start | bytes 331784
  537.1 75.3 %copy-start.1 = (bf16[128,2304]{1,0:T(8,128)(2,1)S(1)}, bf16[128,2304]{1,0:T(8,128)(2,1)}, u32[]{:S(2)}) copy-start(bf16[128,2304]{1,0:T(8,128)(2,1)} %param.12) | copy-start | bytes 1769476
  (1 other events, 1.2 us)
Sparse Core Ops, SparseCore 0:
  11.2 81.9 all-gather.5
  95.7 230.1 all-gather.3
  541.2 69.2 all-reduce.5
where the time goes:
time: 620 us; the launch traced here: 619 us
  blocking collectives  326 us (53%)
  waiting for transfers between devices  85.8 us (14%)
  local copies, waits for them, and re-layouts  66.8 us (11%)
  other arithmetic  52.7 us (8%)
  starting transfers between devices  40.2 us (6%)
  matrix products  31.2 us (5%)
  between operations  16.1 us (3%)
    unnamed x2, blocking collectives  226 us
    psum x1, blocking collectives, body(): lax.psum((jnp.sum(squares, axis=0), jnp.sum(row_new)), ('dp', 'vocab'))  74.8 us
    psum x1, waiting for transfers between devices, body(): next_rows = lax.psum(spread.astype(jnp.bfloat16), 'vocab')  64.9 us
    unnamed x5, other arithmetic  31.9 us
    unnamed x6, starting transfers between devices  28.6 us
    all_to_all x3, local copies, waits for them, and re-layouts, body(): lax.all_to_all(slopes, 'dp', split_axis=1, concat_axis=0, tiled=True)  25.3 us
    gather x1, local copies, waits for them, and re-layouts, body(): mapped = vocab_map[target_ids] - vocab_index * shard_cols  23 us
    dot_general x1, matrix products, body(): jnp.einsum('tv,td->vd', owned_slopes, lax.all_gather(hidden, 'dp', axis=0...  18.5 us
  transfers between devices with their start and end apart: 10, of which 4 were waited for; matrix products, arithmetic and copies ran while one was open for 19% of the time, Pallas kernels for 0%

commit v1 on v0

--- a/solution.py
+++ b/solution.py
@@ -1,3 +1,4 @@
+import functools
 import jax
 import jax.numpy as jnp
 from jax import lax
@@ -6,6 +7,13 @@
 DECAY_RATE = 0.9
 STEP_SCALE = 0.01
 SQUARE_EPS = 1e-30
+
+
+def tell_tables(field_in, lane_axis, along_axis):
+    return jax.lax.psum(jax.lax.psum(field_in, lane_axis), along_axis)
+
+
+kinds_assign = functools.partial(tell_tables, lane_axis="dp", along_axis="vocab")
 
 
 def body(
@@ -75,9 +83,7 @@
     grad = head_grad + jnp.dot(matches, all_cot, preferred_element_type=jnp.float32)
     squares = grad * grad + SQUARE_EPS
     row_new = DECAY_RATE * row_moment + (1.0 - DECAY_RATE) * jnp.mean(squares, axis=1)
-    column_total, row_total = lax.psum(
-        (jnp.sum(squares, axis=0), jnp.sum(row_new)), ("dp", "vocab")
-    )
+    column_total, row_total = kinds_assign((jnp.sum(squares, axis=0), jnp.sum(row_new)))
     vocab_rows = owned_rows * dp_count * vocab_count
     col_new = DECAY_RATE * col_moment + (1.0 - DECAY_RATE) * (column_total / vocab_rows)
     scale = row_new[:, None] * col_new[None, :] / (row_total / vocab_rows)

time: 620 us -> 707 us (1.14)
  blocking collectives: 326 us -> 415 us
    psum x1 -> x2, blocking collectives: 74.8 us -> 154 us  [tell_tables(): return jax.lax.psum(jax.lax.psum(field_in, lane_axis), along_axis)]
    unnamed x2, blocking collectives: 226 us -> 235 us
  transfers between devices with their start and end apart: 10 -> 10, of which waited for: 4 -> 3; matrix products, arithmetic and copies ran while one was open for 19% -> 17% of each run, Pallas kernels for 0% -> 0%
where the time goes in v1:
time: 707 us; the launch traced here: 706 us
  blocking collectives  415 us (59%)
  waiting for transfers between devices  84.9 us (12%)
  local copies, waits for them, and re-layouts  66.8 us (9%)
  other arithmetic  52.7 us (7%)
  starting transfers between devices  39.4 us (6%)
  matrix products  31.2 us (4%)
  between operations  16.1 us (2%)
    unnamed x2, blocking collectives  235 us
    psum x2, blocking collectives, tell_tables(): return jax.lax.psum(jax.lax.psum(field_in, lane_axis), along_axis)  154 us
    psum x1, waiting for transfers between devices, body(): next_rows = lax.psum(spread.astype(jnp.bfloat16), 'vocab')  64.1 us
    unnamed x5, other arithmetic  31.9 us
    unnamed x6, starting transfers between devices  27.7 us
    all_to_all x3, local copies, waits for them, and re-layouts, body(): lax.all_to_all(slopes, 'dp', split_axis=1, concat_axis=0, tiled=True)  25.3 us
    gather x1, local copies, waits for them, and re-layouts, body(): mapped = vocab_map[target_ids] - vocab_index * shard_cols  23 us
    dot_general x1, matrix products, body(): jnp.einsum('tv,td->vd', owned_slopes, lax.all_gather(hidden, 'dp', axis=0...  18.5 us
  transfers between devices with their start and end apart: 10, of which 3 were waited for; matrix products, arithmetic and copies ran while one was open for 17% of the time, Pallas kernels for 0%

profile of v1, /device:TPU:8, one launch (start us, length us, event | category | flops | bytes accessed | tf_op | source)
XLA Modules:
  0.0 705.7 jit_solution(5819675606144294466)
XLA Ops:
  11.0 23.0 %gather_fusion = s32[4096]{0:T(1024)S(1)} fusion(s32[128256]{0:T(1024)S(1)} %copy-done.2, s32[4096]{0:T(1024)S(1)} %broadcast_clamp_fusion), kind=kCustom, calls=%fused_computation | custom fusion | bytes 49152 | tf_op jit(solution)/shard_map/gather | solution.py:45
  35.2 31.6 %scatter_custom_fusion = f32[2048000]{0:T(1024)} fusion(s32[4096]{0:T(1024)S(1)} %reshape.100, f32[4096]{0:T(1024)S(1)} %reshape.102, f32[]{:T(128)} %constant.21.clone.1), kind=kCustom, calls=%fused_computation.10 | custom fusion | flops 4096 | bytes 8192004
  66.8 9.1 %reshape.90 = f32[128,16000]{1,0:T(8,128)} reshape(f32[2048000]{0:T(1024)} %scatter_custom_fusion) | data formatting | bytes 16384000 | tf_op jit(solution)/shard_map/scatter-add | solution.py:53
  78.8 13.1 %pmax.7 = f32[128]{0:T(128)S(1)} all-reduce(bf16[128]{0:T(256)(128)(2,1)S(1)} %reduce_max.23), channel_id=1, replica_groups=mesh['dp'=32,'vocab'=8] {'vocab'}, use_global_device_ids=true, to_apply=%region_1.0 | all-reduce | flops 128 | bytes 768 | tf_op jit(solution)/shard_map/pmax | solution.py:39
  91.9 3.7 fusion.1
  95.5 12.4 %psum.42 = f32[128]{0:T(128)S(1)} all-reduce(f32[128]{0:T(128)S(1)} %fusion.1), channel_id=1, replica_groups=mesh['dp'=32,'vocab'=8] {'vocab'}, use_global_device_ids=true, to_apply=%region_3.0 | all-reduce | flops 128 | bytes 1024 | tf_op jit(solution)/shard_map/psum | solution.py:40
  108.0 6.9 subtract_convert_fusion
  114.9 10.9 %reshape.126 = bf16[128,32,500]{2,1,0:T(8,128)(2,1)} reshape(bf16[128,16000]{1,0:T(8,128)(2,1)} %subtract_convert_fusion) | data formatting | bytes 8192000 | tf_op jit(solution)/shard_map/all_to_all | solution.py:56
  125.7 7.9 %copy.40 = bf16[128,32,500]{0,2,1:T(8,128)(2,1)} copy(bf16[128,32,500]{2,1,0:T(8,128)(2,1)} %reshape.126) | data formatting | bytes 8192000 | tf_op jit(solution)/shard_map/all_to_all | solution.py:56
  133.6 11.5 %all-to-all-start = ((bf16[128,32,500]{0,2,1:T(8,128)(2,1)}), bf16[128,32,500]{0,2,1:T(8,128)(2,1)}, u32[]{:S(2)}, u32[]{:S(2)}) async-start(bf16[128,32,500]{0,2,1:T(8,128)(2,1)} %copy.40), calls=%async_computation | async-start | bytes 8257536 | tf_op jit(solution)/shard_map/all_to_all | solution.py:56
  146.8 146.2 %all-reduce = s32[640]{0:T(1024)S(1)} all-reduce(s32[640]{0:T(1024)S(1)} %select_dynamic-update-slice_fusion), channel_id=1, replica_groups=mesh['dp'=32,'vocab'=8] {'dp'}, use_global_device_ids=true, to_apply=%add | all-reduce | flops 640 | bytes 5120
  293.0 3.8 reshape.123
  296.8 4.1 fusion.8
  301.0 6.6 copy.38
  307.5 18.4 %all-gather.4.cloned.1.call-done = bf16[4096,2304]{1,0:T(8,128)(2,1)} async-done(((bf16[128,2304]{1,0:T(8,128)(2,1)}), bf16[4096,2304]{1,0:T(8,128)(2,1)}) %all-gather.4.cloned.1.call-update) | async-done | bytes 18874384 | tf_op jit(solution)/shard_map/all_gather | solution.py:60
  326.0 18.5 %fusion.4 = (f32[2304]{0:T(1024)S(1)}, f32[500]{0:T(512)S(1)}, f32[500,2304]{1,0:T(8,128)}) fusion(f32[500,2304]{1,0:T(8,128)} %fusion.8, bf16[4096,500]{1,0:T(8,128)(2,1)} %bitcast.14, bf16[4096,2304]{1,0:T(8,128)(2,1)} %all-gather.4.cloned.1.call-done), kind=kOutput, calls=%fused_computation.12 | convolution fusion | flops 9442941952 | bytes 32197584 | tf_op jit(solution)/shard_map/tv,td->vd/dot_general | solution.py:57
  345.1 129.5 %all-reduce.3 = (f32[]{:T(128)}, f32[2304]{0:T(1024)S(1)}) all-reduce(f32[]{:T(128)} %get-tuple-element.10, f32[2304]{0:T(1024)S(1)} %get-tuple-element.4), channel_id=1, replica_groups=mesh['dp'=32,'vocab'=8] {'dp'}, use_global_device_ids=true, to_apply=%region_15.16 | all-reduce | flops 2305 | bytes 18440 | tf_op jit(solution)/shard_map/psum | solution.py:13
  474.6 24.6 %all-reduce.4 = (f32[]{:T(128)}, f32[2304]{0:T(1024)S(1)}) all-reduce(f32[]{:T(128)} %get-tuple-element.6, f32[2304]{0:T(1024)S(1)} %get-tuple-element.7), channel_id=1, replica_groups=mesh['dp'=32,'vocab'=8] {'vocab'}, use_global_device_ids=true, to_apply=%region_16.17 | all-reduce | flops 2305 | bytes 18440 | tf_op jit(solution)/shard_map/psum | solution.py:13
  499.9 5.8 convolution_convert_fusion
  505.7 88.9 %fusion = bf16[24,2304]{1,0:T(8,128)(2,1)S(1)} fusion(bf16[640,2304]{1,0:T(8,128)(2,1)S(1)} %convolution_convert_fusion), kind=kCustom, calls=%all-reduce-scatter | all-reduce-scatter fusion | flops 1769473 | bytes 3060736
  602.3 8.5 %collective-permute-start.3 = (bf16[24,2304]{1,0:T(8,128)(2,1)S(1)}, bf16[24,2304]{1,0:T(8,128)(2,1)S(1)}, u32[]{:S(2)}, u32[]{:S(2)}) collective-permute-start(bf16[24,2304]{1,0:T(8,128)(2,1)S(1)} %fusion), channel_id=1, source_target_pairs={{0,32},{8,40},{16,48},{24,56},{32,64},{40,72},{48,80},{56,88},{64,... | collective-permute-start | bytes 331784
  610.8 11.6 %collective-permute-start.4 = (bf16[24,2304]{1,0:T(8,128)(2,1)S(1)}, bf16[24,2304]{1,0:T(8,128)(2,1)S(1)}, u32[]{:S(2)}, u32[]{:S(2)}) collective-permute-start(bf16[24,2304]{1,0:T(8,128)(2,1)S(1)} %fusion), channel_id=1, source_target_pairs={{0,40},{8,48},{16,56},{24,64},{32,72},{40,80},{48,88},{56,96},{64,... | collective-permute-start | bytes 331784
  628.7 4.5 fusion.23
  633.2 64.1 %all-reduce.7.cloned.1.call-done = bf16[128,2304]{1,0:T(8,128)(2,1)} async-done(((bf16[128,2304]{1,0:T(8,128)(2,1)}), bf16[128,2304]{1,0:T(8,128)(2,1)}) %all-reduce.7.cloned.1.call-update) | async-done | bytes 589840 | tf_op jit(solution)/shard_map/psum | solution.py:101
  (87 shorter events, 24.6 us)
Async XLA Ops:
  7.2 3.8 copy-start.2
  7.2 285.8 %all-gather.6.cloned.1.call-start = ((), (), s32[]{:S(2)}) async-start(), calls=%async_computation.3 | async-start | bytes 3649536 | tf_op jit(solution)/shard_map/all_gather | solution.py:78
  8.0 138.6 %copy-start.9 = (pred[128]{0:T(512)(128)(4,1)}, pred[128]{0:T(512)(128)(4,1)S(1)}, u32[]{:S(2)}) copy-start(pred[128]{0:T(512)(128)(4,1)S(1)} %get-tuple-element.13) | copy-start | bytes 388
  8.4 138.2 %copy-start.8 = (s32[128]{0:T(128)}, s32[128]{0:T(128)S(1)}, u32[]{:S(2)}) copy-start(s32[128]{0:T(128)S(1)} %add_reduce_fusion) | copy-start | bytes 1540
  9.3 316.7 %all-gather.4.cloned.1.call-start = ((), (), s32[]{:S(2)}) async-start(), calls=%async_computation.1 | async-start | bytes 19464192 | tf_op jit(solution)/shard_map/all_gather | solution.py:60
  11.0 23.3 %copy-start.14 = (s32[2]{0:T(128)S(1)}, s32[2]{0:T(128)}, u32[]{:S(2)}) copy-start(s32[2]{0:T(128)} %constant.64) | copy-start | bytes 28
  11.0 23.3 %copy-start.13 = (s32[2]{0:T(128)S(1)}, s32[2]{0:T(128)}, u32[]{:S(2)}) copy-start(s32[2]{0:T(128)} %constant.67) | copy-start | bytes 28
  11.0 23.7 %copy-start.4 = (f32[128,32]{0,1:T(8,128)S(1)}, f32[128,32]{0,1:T(8,128)}, u32[]{:S(2)}) copy-start(f32[128,32]{0,1:T(8,128)} %param.15) | copy-start | bytes 49156
  133.6 11.6 %copy-start.12 = (u32[256]{0:T(256)S(1)}, u32[256]{0:T(256)}, u32[]{:S(2)}) copy-start(u32[256]{0:T(256)} %constant.74) | copy-start | bytes 3076
  133.6 13.0 %copy-start.11 = (s32[128]{0:T(128)S(1)}, s32[128]{0:T(128)}, u32[]{:S(2)}) copy-start(s32[128]{0:T(128)} %param.13) | copy-start | bytes 1540
  133.6 167.3 %all-to-all-start = ((bf16[128,32,500]{0,2,1:T(8,128)(2,1)}), bf16[128,32,500]{0,2,1:T(8,128)(2,1)}, u32[]{:S(2)}, u32[]{:S(2)}) async-start(bf16[128,32,500]{0,2,1:T(8,128)(2,1)} %copy.40), calls=%async_computation | async-start | bytes 8257536 | tf_op jit(solution)/shard_map/all_to_all | solution.py:56
  145.2 552.1 %all-reduce.7.cloned.1.call-start = ((), (), s32[]{:S(2)}) async-start(), calls=%async_computation.2 | async-start | bytes 1179648 | tf_op jit(solution)/shard_map/psum | solution.py:101
  326.0 18.5 %copy-start.10 = (f32[500]{0:T(512)S(1)}, f32[500]{0:T(512)}, u32[]{:S(2)}) copy-start(f32[500]{0:T(512)} %param.18) | copy-start | bytes 6004
  326.0 173.2 %copy-start.6 = (f32[2304]{0:T(1024)S(1)}, f32[2304]{0:T(1024)}, u32[]{:S(2)}) copy-start(f32[2304]{0:T(1024)} %param.19) | copy-start | bytes 27652
  345.1 283.6 %copy-start.7 = (f32[500]{0:T(512)}, f32[500]{0:T(512)S(1)}, u32[]{:S(2)}) copy-start(f32[500]{0:T(512)S(1)} %get-tuple-element.18) | copy-start | bytes 6004
  499.2 129.5 %copy-start.5 = (f32[2304]{0:T(1024)}, f32[2304]{0:T(1024)S(1)}, u32[]{:S(2)}) copy-start(f32[2304]{0:T(1024)S(1)} %multiply_add_fusion.1) | copy-start | bytes 27652
  594.6 28.5 %copy-start.3 = (bf16[24,2304]{1,0:T(8,128)(2,1)}, bf16[24,2304]{1,0:T(8,128)(2,1)S(1)}, u32[]{:S(2)}) copy-start(bf16[24,2304]{1,0:T(8,128)(2,1)S(1)} %fusion) | copy-start | bytes 331780
  594.6 16.2 %collective-permute-start.5 = (bf16[4,2304]{1,0:T(4,128)(2,1)S(1)}, bf16[4,2304]{1,0:T(4,128)(2,1)S(1)}, u32[]{:S(2)}, u32[]{:S(2)}) collective-permute-start(bf16[4,2304]{1,0:T(4,128)(2,1)S(1)} %slice.2), channel_id=1, source_target_pairs={{0,48},{8,56},{16,64},{24,72},{32,80},{40,88},{48,96},{56,104},{64... | collective-permute-start | bytes 55304
  596.5 26.5 %collective-permute-start = (bf16[24,2304]{1,0:T(8,128)(2,1)S(1)}, bf16[24,2304]{1,0:T(8,128)(2,1)S(1)}, u32[]{:S(2)}, u32[]{:S(2)}) collective-permute-start(bf16[24,2304]{1,0:T(8,128)(2,1)S(1)} %fusion), channel_id=1, source_target_pairs={{0,8},{8,16},{16,24},{24,32},{32,40},{40,48},{48,56},{56,64},{64,7... | collective-permute-start | bytes 331784
  598.5 24.6 %collective-permute-start.1 = (bf16[24,2304]{1,0:T(8,128)(2,1)S(1)}, bf16[24,2304]{1,0:T(8,128)(2,1)S(1)}, u32[]{:S(2)}, u32[]{:S(2)}) collective-permute-start(bf16[24,2304]{1,0:T(8,128)(2,1)S(1)} %fusion), channel_id=1, source_target_pairs={{0,16},{8,24},{16,32},{24,40},{32,48},{40,56},{48,64},{56,72},{64,... | collective-permute-start | bytes 331784
  600.4 22.7 %collective-permute-start.2 = (bf16[24,2304]{1,0:T(8,128)(2,1)S(1)}, bf16[24,2304]{1,0:T(8,128)(2,1)S(1)}, u32[]{:S(2)}, u32[]{:S(2)}) collective-permute-start(bf16[24,2304]{1,0:T(8,128)(2,1)S(1)} %fusion), channel_id=1, source_target_pairs={{0,24},{8,32},{16,40},{24,48},{32,56},{40,64},{48,72},{56,80},{64,... | collective-permute-start | bytes 331784
  602.3 20.8 %collective-permute-start.3 = (bf16[24,2304]{1,0:T(8,128)(2,1)S(1)}, bf16[24,2304]{1,0:T(8,128)(2,1)S(1)}, u32[]{:S(2)}, u32[]{:S(2)}) collective-permute-start(bf16[24,2304]{1,0:T(8,128)(2,1)S(1)} %fusion), channel_id=1, source_target_pairs={{0,32},{8,40},{16,48},{24,56},{32,64},{40,72},{48,80},{56,88},{64,... | collective-permute-start | bytes 331784
  610.8 13.9 %collective-permute-start.4 = (bf16[24,2304]{1,0:T(8,128)(2,1)S(1)}, bf16[24,2304]{1,0:T(8,128)(2,1)S(1)}, u32[]{:S(2)}, u32[]{:S(2)}) collective-permute-start(bf16[24,2304]{1,0:T(8,128)(2,1)S(1)} %fusion), channel_id=1, source_target_pairs={{0,40},{8,48},{16,56},{24,64},{32,72},{40,80},{48,88},{56,96},{64,... | collective-permute-start | bytes 331784
  624.7 74.5 %copy-start.1 = (bf16[128,2304]{1,0:T(8,128)(2,1)S(1)}, bf16[128,2304]{1,0:T(8,128)(2,1)}, u32[]{:S(2)}) copy-start(bf16[128,2304]{1,0:T(8,128)(2,1)} %param.12) | copy-start | bytes 1769476
  (1 other events, 1.2 us)
Sparse Core Ops, SparseCore 0:
  11.2 81.9 all-gather.5
  95.7 230.1 all-gather.3
  628.8 68.4 all-reduce.6
